TPU v7x, 32 devices: a whole 2x2x4 slice. The times are simulated.
32 devices in a mesh: shard: 2 (over y), tensor: 4 (over z), section: 4 (over x, core).
Axes of the slice: x: 2, y: 2, z: 4, core: 2. Of those that a mesh axis runs over, the one named last changes fastest.
Arguments:
- xin: bfloat16 [4, 16384, 768], P(None, ('shard', 'tensor', 'section')), may hold values from -6 to 6
- dout: bfloat16 [4, 16384, 768], P(None, ('shard', 'tensor', 'section')), may hold values from -6 to 6
- weights: bfloat16 [4, 768, 768], P(None, ('tensor', 'section')), may hold values from -0.21875 to 0.21875
- slot_block: int32 [8], replicated, may hold values from -1 to 3, as said below
- left_stat: float32 [8, 768, 768], P('shard', ('tensor', 'section')), may hold values from -1 to 10, as said below
- right_stat: float32 [8, 768, 768], P('shard', ('tensor', 'section')), may hold values from -1 to 10, as said below
- left_root: float32 [8, 768, 768], P('shard', ('tensor', 'section')), may hold values from -1 to 10, as said below
- right_root: float32 [8, 768, 768], P('shard', ('tensor', 'section')), may hold values from -1 to 10, as said below
- first_moment: float32 [8, 768, 768], P('shard', ('tensor', 'section')), may hold values from -0.3 to 0.3
- second_moment: float32 [8, 768, 768], P('shard', ('tensor', 'section')), may hold values from 0.001 to 0.01
Outputs:
- new_weights: bfloat16 [4, 768, 768], P(None, ('tensor', 'section'))
- new_left: float32 [8, 768, 768], P('shard', ('tensor', 'section'))
- new_right: float32 [8, 768, 768], P('shard', ('tensor', 'section'))
- new_first: float32 [8, 768, 768], P('shard', ('tensor', 'section'))
- new_second: float32 [8, 768, 768], P('shard', ('tensor', 'section'))
Inputs may be any that keep to these rules, and one draw needn't show every extreme that they name: `slot_block`: every block 0 to 3 stands in exactly one slot; slots 4 s to 4 s + 3 belong to shard index s; some shard index holds two blocks and none holds more; the other slots hold -1. `left_stat`: each slot is a symmetric positive definite matrix. `right_stat`: each slot is a symmetric positive definite matrix. `left_root`: each slot is a symmetric positive definite matrix. `right_root`: each slot is a symmetric positive definite matrix.
All inputs are finite; a program needn't handle non-finite values.
Results may differ from a plain program's by a relative error of at most 0.00045.
Values may be sent and summed in bfloat16 or wider, within the bound.
No kernel may reach another device: no remote copies, remote signals or barrier semaphores. Data moves between devices by JAX's collectives and lax.ppermute only.
A program may use at most 128 MiB of HBM per device.

v0:
```python
import math
import jax
import jax.numpy as jnp
from jax import lax
from jax.sharding import PartitionSpec as P


def spread(value, axis, source):
    kept = jnp.where(lax.axis_index(axis) == source, value, 0).astype(value.dtype)
    return lax.psum(kept, axis)


def absorb_slot(mine_rows, root_rows, portion, col_first):
    highest = lax.Precision.HIGHEST
    row_count = mine_rows.shape[0]
    block_part = jnp.dot(mine_rows, portion.T, precision=highest)
    own_cols = lax.dynamic_slice_in_dim(portion, col_first, row_count, 1)
    right_gram = jnp.dot(own_cols.T, portion, precision=highest)
    left_prod = jnp.dot(root_rows, portion, precision=highest)
    return (block_part, right_gram, left_prod)


def apply_slot(prod_rows, portion):
    return jnp.dot(prod_rows, portion, precision=lax.Precision.HIGHEST)


def on_device(
    xin,
    dout,
    weights,
    slot_block,
    left_stat,
    right_stat,
    left_root,
    right_root,
    first_moment,
    second_moment,
):
    block_count, tok_count, block_size = xin.shape
    slot_count, row_count = (left_stat.shape[0], left_stat.shape[1])
    group_count = lax.axis_size(("tensor", "section"))
    shard_count = lax.axis_size("shard")
    factor = 1.0 / math.sqrt(tok_count * shard_count * group_count * block_size)
    pieces_out = []
    for grad_member in range(block_count):
        cols = xin[grad_member]
        pieces_out.append(
            jnp.einsum("tr,tc->rc", cols, dout[grad_member], preferred_element_type=jnp.float32)
        )
    partial_rows = lax.psum_scatter(
        jnp.concatenate(pieces_out, axis=1) * factor,
        ("tensor", "section"),
        scatter_dimension=0,
        tiled=True,
    )
    grad_rows = lax.psum(partial_rows, "shard")
    shard_idx = lax.axis_index("shard")
    group_idx = lax.axis_index(("tensor", "section"))
    my_slots = lax.dynamic_slice_in_dim(slot_block, shard_idx * slot_count, slot_count)
    valid = my_slots >= 0
    picks = jnp.maximum(my_slots, 0)
    grad_three = grad_rows.reshape(row_count, block_count, block_size)
    mine = jnp.moveaxis(jnp.take(grad_three, picks, axis=1), 1, 0)
    col_first = group_idx * row_count
    zeros_rows = jnp.zeros((slot_count, row_count, block_size), jnp.float32)
    totals = (zeros_rows, zeros_rows, zeros_rows)
    portion = lax.all_gather(mine, ("tensor", "section"), axis=1, tiled=True)
    lefts = []
    rights = []
    prods = []
    for slot_pos in range(slot_count):
        current = (totals[0][slot_pos], totals[1][slot_pos], totals[2][slot_pos])
        result = lax.cond(
            valid[slot_pos],
            lambda values: absorb_slot(
                mine[slot_pos], left_root[slot_pos], portion[slot_pos], col_first
            ),
            lambda values: values,
            current,
        )
        lefts.append(result[0])
        rights.append(result[1])
        prods.append(result[2])
    left_gram = jnp.stack(lefts)
    right_gram = jnp.stack(rights)
    left_prod = jnp.stack(prods)
    apply_portion = lax.all_gather(right_root, ("tensor", "section"), axis=1, tiled=True)
    outputs = []
    for apply_slot_pos in range(slot_count):
        outputs.append(
            lax.cond(
                valid[apply_slot_pos],
                lambda values: apply_slot(left_prod[apply_slot_pos], apply_portion[apply_slot_pos]),
                lambda values: values,
                zeros_rows[apply_slot_pos],
            )
        )
    direction = jnp.stack(outputs)
    moment_one = 0.9 * first_moment + 0.1 * mine
    moment_two = 0.999 * second_moment + 0.001 * mine * mine
    adam = moment_one / (jnp.sqrt(moment_two) + 1e-08)
    adam_sq, dir_sq = lax.psum(
        (jnp.sum(adam * adam, axis=(1, 2)), jnp.sum(direction * direction, axis=(1, 2))),
        ("tensor", "section"),
    )
    graft = jnp.sqrt(adam_sq) / (jnp.sqrt(dir_sq) + 1e-06)
    mask = valid[:, None, None]
    new_left = jnp.where(mask, 0.5 * left_stat + 0.5 * left_gram, left_stat)
    new_right = jnp.where(mask, 0.5 * right_stat + 0.5 * right_gram, right_stat)
    new_first = jnp.where(mask, moment_one, first_moment)
    new_second = jnp.where(mask, moment_two, second_moment)
    my_weights = jnp.take(weights, picks, axis=0)
    new_rows = (my_weights.astype(jnp.float32) - 0.05 * graft[:, None, None] * direction).astype(
        jnp.bfloat16
    )
    slot_ids = jnp.arange(slot_block.shape[0], dtype=jnp.int32)
    holders = [
        jnp.sum(slot_ids * (slot_block == member).astype(jnp.int32))
        for member in range(block_count)
    ]
    published = []
    for member in range(block_count):
        owner = holders[member] // slot_count
        within = holders[member] % slot_count
        chosen = lax.dynamic_index_in_dim(new_rows, within, 0, keepdims=False)
        published.append(spread(chosen, "shard", owner))
    new_weights = jnp.stack(published)
    return (new_weights, new_left, new_right, new_first, new_second)


def solution(mesh):
    placed = (
        P(None, ("shard", "tensor", "section"), None),
        P(None, ("shard", "tensor", "section"), None),
        P(None, ("tensor", "section"), None),
        P(),
        P("shard", ("tensor", "section"), None),
        P("shard", ("tensor", "section"), None),
        P("shard", ("tensor", "section"), None),
        P("shard", ("tensor", "section"), None),
        P("shard", ("tensor", "section"), None),
        P("shard", ("tensor", "section"), None),
    )
    return jax.shard_map(
        on_device,
        mesh=mesh,
        in_specs=placed,
        out_specs=(
            P(None, ("tensor", "section"), None),
            P("shard", ("tensor", "section"), None),
            P("shard", ("tensor", "section"), None),
            P("shard", ("tensor", "section"), None),
            P("shard", ("tensor", "section"), None),
        ),
        check_vma=False,
    )
```

profile of v0, /device:TPU:0, one launch (start us, length us, event | category | flops | bytes accessed | tf_op | source)
XLA Modules:
  0.0 413.0 jit_solution(5907693126761822649)
XLA Ops:
  7.2 0.0 copy-start
  7.2 0.0 copy-start.3
  7.2 0.0 reduce-scatter.4.cloned.1.call-start
  7.2 2.4 fusion.108
  9.6 0.0 copy-start.4
  9.6 2.1 fusion.111
  11.8 0.8 fusion.114
  12.6 0.8 fusion.117
  13.4 4.1 maximum_multiply_fusion
  17.5 9.7 %copy.20 = f32[768,3072]{1,0:T(8,128)} copy(f32[768,3072]{0,1:T(8,128)} %maximum_multiply_fusion) | data formatting | bytes 18874368
  27.2 0.0 reduce-scatter.4.cloned.1.call-update
  27.2 0.0 copy-start.14
  27.2 0.0 all-reduce.5.cloned.1.call-start
  27.2 114.2 %reduce-scatter.4.cloned.1.call-done = f32[48,3072]{1,0:T(8,128)} async-done(((f32[768,3072]{1,0:T(8,128)}), f32[48,3072]{1,0:T(8,128)}) %reduce-scatter.4.cloned.1.call-update) | async-done | bytes 589840
  141.4 1.5 copy.21
  142.9 0.0 copy-start.5
  142.9 1.3 copy.17
  144.2 0.0 all-reduce.5.cloned.1.call-update
  144.2 0.0 all-gather.5.cloned.1.call-start
  144.3 0.1 broadcast_compare_fusion
  144.4 29.8 %all-reduce.5.cloned.1.call-done = f32[48,4,768]{2,0,1:T(8,128)} async-done(((f32[48,4,768]{2,0,1:T(8,128)}), f32[48,4,768]{2,0,1:T(8,128)}) %all-reduce.5.cloned.1.call-update) | async-done | bytes 589840 | tf_op jit(solution)/shard_map/psum | solution.py:56
  174.2 1.6 gather_fusion.1
  175.9 1.2 fusion.134
  177.1 0.0 all-gather.5.cloned.1.call-update
  177.1 0.0 all-gather.3.cloned.1.call-start
  177.1 0.5 all-gather.3.cloned.1.call-update
  177.7 0.0 all-reduce.7.cloned.1.call-start
  177.7 0.7 fusion.135
  188.8 0.6 fusion.140
  192.0 0.6 gather_fusion
  192.7 66.0 %all-gather.5.cloned.1.call-done = f32[4,768,768]{2,1,0:T(8,128)} async-done(((f32[4,48,768]{2,1,0:T(8,128)}), f32[4,768,768]{2,1,0:T(8,128)}) %all-gather.5.cloned.1.call-update) | async-done | bytes 9437200 | tf_op jit(solution)/shard_map/all_gather | solution.py:67
  258.7 0.1 conditional.8
  258.8 11.2 %conditional.10 = (f32[48,768]{1,0:T(8,128)S(1)}, f32[1,48,768]{2,1,0:T(8,128)S(1)}, f32[1,48,768]{2,1,0:T(8,128)S(1)}) conditional(s32[]{:T(128)} %bitcast.42, () %tuple.93, (f32[4,48,768]{2,1,0:T(8,128)}, f32[4,768,768]{2,1,0:T(8,128)}, f32[4,48,768]{2,1,0:T(8,128)}, s32[]{:T(128)}) %tuple.90), branch_computations={%region_9.10_spmd, %region_10.11_spmd} | conditional | flops 1019215872 | bytes 12927038 | solution.py:73
  259.0 1.8 slice.65
  260.8 1.7 fusion.36
  262.5 3.3 fusion.31
  265.7 4.2 %fusion.33 = f32[1,48,768]{2,1,0:T(8,128)S(1)} fusion(f32[4,48,768]{2,1,0:T(8,128)} %get-tuple-element.80, f32[4,768,768]{2,1,0:T(8,128)} %get-tuple-element.79), kind=kOutput, calls=%fused_computation.29 | convolution fusion | flops 339738624 | bytes 2654208 | tf_op jit(solution)/shard_map/cond/branch_1_fun/dot_general | solution.py:16
  270.0 0.6 copy-done.7
  270.7 0.1 conditional.12
  270.7 0.6 copy-done.8
  271.4 0.1 copy-done.9
  271.4 10.8 %conditional.14 = (f32[48,768]{1,0:T(8,128)S(1)}, f32[1,48,768]{2,1,0:T(8,128)S(1)}, f32[1,48,768]{2,1,0:T(8,128)S(1)}) conditional(s32[]{:T(128)} %bitcast.44, () %tuple.99, (f32[4,48,768]{2,1,0:T(8,128)}, f32[4,768,768]{2,1,0:T(8,128)}, f32[4,48,768]{2,1,0:T(8,128)}, s32[]{:T(128)}) %tuple.90), branch_computations={%region_17.18_spmd, %region_18.19_spmd} | conditional | flops 1019215872 | bytes 12927038 | solution.py:73
  271.4 1.8 slice.73
  273.3 1.7 fusion.90
  275.0 3.3 fusion.85
  278.2 4.0 fusion.87
  282.3 0.0 copy-start.12
  282.3 58.2 %all-gather.3.cloned.1.call-done = f32[4,768,768]{2,1,0:T(8,128)} async-done(((f32[4,48,768]{2,1,0:T(8,128)}), f32[4,768,768]{2,1,0:T(8,128)}) %all-gather.3.cloned.1.call-update) | async-done | bytes 9437200 | tf_op jit(solution)/shard_map/all_gather | solution.py:87
  340.5 3.2 conditional.11
  340.5 3.2 fusion.51
  343.7 0.0 copy-start.13
  343.8 0.0 copy-start.2
  343.8 0.0 copy-start.6
  343.8 0.8 copy-done.13
  344.6 3.2 conditional.15
  344.6 3.2 fusion.105
  347.8 0.2 multiply_reduce_fusion
  348.0 3.3 fusion.133
  351.3 30.8 %all-reduce = (f32[4]{0:T(128)S(1)}, f32[4]{0:T(128)S(1)}) all-reduce(f32[4]{0:T(128)S(1)} %multiply_reduce_fusion, f32[4]{0:T(128)S(1)} %get-tuple-element.140), channel_id=1, replica_groups=mesh['shard'=2,'tensor'=4,'section'=4] {'tensor','section'}, use_global_device_ids=true, to_apply=%region_22.23 | all-reduce | flops 8 | bytes 64 | tf_op jit(solution)/shard_map/psum | solution.py:102
  382.2 0.2 subtract_convert_fusion
  382.3 0.7 dynamic-slice_select_fusion.3
  383.0 0.0 all-reduce.7.cloned.1.call-update
  383.1 21.7 %all-reduce.7.cloned.1.call-done = (bf16[1,48,768]{2,1,0:T(8,128)(2,1)}, bf16[1,48,768]{2,1,0:T(8,128)(2,1)}, bf16[1,48,768]{2,1,0:T(8,128)(2,1)}, bf16[1,48,768]{2,1,0:T(8,128)(2,1)}) async-done(((bf16[1,48,768]{2,1,0:T(8,128)(2,1)}, bf16[1,48,768]{2,1,0:T(8,128)(2,1)}, bf16[1,48,768]{2,1,0:T(8,128)(2,1)}, bf16[1,48,768]{2,1,0:T(8,128)(2,1)}), (bf16[1,48,768]{2,1,0:T(8,128)(2,1)}, ...) | async-done | bytes 294928 | tf_op jit(solution)/shard_map/psum | solution.py:10
  404.7 1.7 pad_maximum_fusion.1
  (29 shorter events, 0.2 us)
Async XLA Ops:
  7.2 184.8 %copy-start = (bf16[4,48,768]{2,1,0:T(8,128)(2,1)S(1)}, bf16[4,48,768]{2,1,0:T(8,128)(2,1)}, u32[]{:S(2)}) copy-start(bf16[4,48,768]{2,1,0:T(8,128)(2,1)} %param.28) | copy-start | bytes 884740
  7.2 2.4 copy-start.3
  7.2 134.2 %reduce-scatter.4.cloned.1.call-start = ((), (), s32[]{:S(2)}) async-start(), calls=%async_computation.4 | async-start | bytes 10027008
  9.6 2.1 copy-start.4
  27.2 117.1 %copy-start.14 = (s32[8]{0:T(128)S(1)}, s32[8]{0:T(128)}, u32[]{:S(2)}) copy-start(s32[8]{0:T(128)} %param.29) | copy-start | bytes 100
  27.2 147.0 %all-reduce.5.cloned.1.call-start = ((), (), s32[]{:S(2)}) async-start(), calls=%async_computation.1 | async-start | bytes 1179648 | tf_op jit(solution)/shard_map/psum | solution.py:56
  142.9 32.9 %copy-start.5 = (f32[4,48,768]{2,1,0:T(8,128)S(1)}, f32[4,48,768]{2,1,0:T(8,128)}, u32[]{:S(2)}) copy-start(f32[4,48,768]{2,1,0:T(8,128)} %param.35) | copy-start | bytes 1769476
  144.2 114.5 %all-gather.5.cloned.1.call-start = ((), (), s32[]{:S(2)}) async-start(), calls=%async_computation.3 | async-start | bytes 10027008 | tf_op jit(solution)/shard_map/all_gather | solution.py:67
  177.1 163.4 %all-gather.3.cloned.1.call-start = ((), (), s32[]{:S(2)}) async-start(), calls=%async_computation.2 | async-start | bytes 10027008 | tf_op jit(solution)/shard_map/all_gather | solution.py:87
  177.7 227.1 %all-reduce.7.cloned.1.call-start = ((), (), s32[]{:S(2)}) async-start(), calls=%async_computation.5 | async-start | bytes 589824 | tf_op jit(solution)/shard_map/psum | solution.py:10
  270.0 0.7 copy-start.7
  270.7 0.7 copy-start.8
  270.7 0.7 copy-start.9
  282.3 61.4 %copy-start.10 = (f32[1,48,768]{2,1,0:T(8,128)}, f32[1,48,768]{2,1,0:T(8,128)S(1)}, u32[]{:S(2)}) copy-start(f32[1,48,768]{2,1,0:T(8,128)S(1)} %get-tuple-element.120) | copy-start | bytes 442372
  282.3 61.4 %copy-start.11 = (f32[1,48,768]{2,1,0:T(8,128)}, f32[1,48,768]{2,1,0:T(8,128)S(1)}, u32[]{:S(2)}) copy-start(f32[1,48,768]{2,1,0:T(8,128)S(1)} %get-tuple-element.124) | copy-start | bytes 442372
  282.3 61.4 %copy-start.12 = (f32[48,768]{1,0:T(8,128)}, f32[48,768]{1,0:T(8,128)S(1)}, u32[]{:S(2)}) copy-start(f32[48,768]{1,0:T(8,128)S(1)} %get-tuple-element.116) | copy-start | bytes 442372
  343.7 0.9 copy-start.13
  343.8 4.2 %copy-start.2 = (f32[4,48,768]{2,1,0:T(8,128)S(1)}, f32[4,48,768]{2,1,0:T(8,128)}, u32[]{:S(2)}) copy-start(f32[4,48,768]{2,1,0:T(8,128)} %get-tuple-element.136) | copy-start | bytes 1769476
  343.8 4.2 %copy-start.6 = (f32[4,48,768]{2,1,0:T(8,128)S(1)}, f32[4,48,768]{2,1,0:T(8,128)}, u32[]{:S(2)}) copy-start(f32[4,48,768]{2,1,0:T(8,128)} %param.34) | copy-start | bytes 1769476
  348.0 58.5 %copy-start.1 = (bf16[4,48,768]{2,1,0:T(8,128)(2,1)S(1)}, bf16[4,48,768]{2,1,0:T(8,128)(2,1)}, u32[]{:S(2)}) copy-start(bf16[4,48,768]{2,1,0:T(8,128)(2,1)} %param.28) | copy-start | bytes 884740
Sparse Core Ops, SparseCore 0:
  27.3 114.0 reduce-scatter.3
  144.4 29.7 all-reduce.4
  177.2 81.4 all-gather.4
  260.9 79.5 all-gather.2
  383.2 21.4 all-reduce.6
where the time goes:
time: 414 us; the launch traced here: 413 us
  waiting for transfers between devices  290 us (70%)
  blocking collectives  30.8 us (7%)
  matrix products  30.6 us (7%)
  between operations  27.2 us (7%)
  local copies, waits for them, and re-layouts  21.3 us (5%)
  other arithmetic  12.2 us (3%)
    unnamed x6, waiting for transfers between devices  115 us
    all_gather x1, waiting for transfers between devices, on_device(): portion = lax.all_gather(mine, ('tensor', 'section'), axis=1, tiled=True)  66 us
    all_gather x1, waiting for transfers between devices, on_device(): lax.all_gather(right_root, ('tensor', 'section'), axis=1, tiled=True)  58.2 us
    psum x1, blocking collectives, on_device(): lax.psum((jnp.sum(adam * adam, axis=(1, 2)), jnp.sum(direction * directio...  30.8 us
    psum x1, waiting for transfers between devices, on_device(): grad_rows = lax.psum(partial_rows, 'shard')  29.8 us
    psum x1, waiting for transfers between devices, spread(): return lax.psum(kept, axis)  21.7 us
    unnamed x32, local copies, waits for them, and re-layouts  13.4 us
    dot_general x2, matrix products, absorb_slot(): block_part = jnp.dot(mine_rows, portion.T, precision=highest)  8.3 us
  transfers between devices with their start and end apart: 5, of which 5 were waited for; matrix products, arithmetic and copies ran while one was open for 6% of the time, Pallas kernels for 0%

commit v1 on v0

--- a/solution.py
+++ b/solution.py
@@ -3,6 +3,34 @@
 import jax.numpy as jnp
 from jax import lax
 from jax.sharding import PartitionSpec as P
+from jax.lax import axis_index, ppermute, psum
+
+
+def edit_cycles_up(frame_in, join_dim):
+    local_now = list(frame_in.shape[1:])
+    local_now[join_dim] *= frame_in.shape[0]
+    taken_in = jnp.moveaxis(frame_in, 0, join_dim).reshape(local_now)
+    return taken_in
+
+
+def try_all_plane_up(m, device_axis):
+    frame_out = psum(1, device_axis)
+    left_arr = axis_index(device_axis)
+    val, q_next = (frame_out, left_arr)
+    row_out, g_now = (m[None], 1)
+    while g_now < val:
+        line_up = []
+        dd = 0
+        while dd < val:
+            line_up.append((dd, dd ^ g_now))
+            dd += 1
+        n_now = ppermute(row_out, device_axis, line_up)
+        p_next = q_next & g_now == 0
+        row_out = jnp.concatenate(
+            [jnp.where(p_next, row_out, n_now), jnp.where(p_next, n_now, row_out)]
+        )
+        g_now *= 2
+    return row_out
 
 
 def spread(value, axis, source):
@@ -64,7 +92,7 @@
     col_first = group_idx * row_count
     zeros_rows = jnp.zeros((slot_count, row_count, block_size), jnp.float32)
     totals = (zeros_rows, zeros_rows, zeros_rows)
-    portion = lax.all_gather(mine, ("tensor", "section"), axis=1, tiled=True)
+    portion = edit_cycles_up(try_all_plane_up(mine, ("tensor", "section")), 1)
     lefts = []
     rights = []
     prods = []

time: 414 us -> 634 us (1.53)
  waiting for transfers between devices: 290 us -> 478 us
  other arithmetic: 12.2 us -> 31.3 us
    ppermute x0 -> x4, waiting for transfers between devices: none -> 311 us  [try_all_plane_up(): n_now = ppermute(row_out, device_axis, line_up)]
    all_gather x1 -> x0, waiting for transfers between devices: 66 us -> none  [on_device(): portion = lax.all_gather(mine, ('tensor', 'section'), axis=1, tiled=True)]
    all_gather x1, waiting for transfers between devices: 58.2 us -> 0.02 us  [on_device(): lax.all_gather(right_root, ('tensor', 'section'), axis=1, tiled=True)]
    select_n x0 -> x4, other arithmetic: none -> 10.8 us  [try_all_plane_up(): jnp.where(p_next, row_out, n_now)]
    unnamed x32 -> x48, local copies, waits for them, and re-layouts: 13.4 us -> 14.7 us
    unnamed x6 -> x5, waiting for transfers between devices: 115 us -> 115 us
  transfers between devices with their start and end apart: 5 -> 8, of which waited for: 5 -> 7; matrix products, arithmetic and copies ran while one was open for 6% -> 8% of each run, Pallas kernels for 0% -> 0%
where the time goes in v1:
time: 634 us; the launch traced here: 633 us
  waiting for transfers between devices  478 us (75%)
  blocking collectives  32.2 us (5%)
  other arithmetic  31.3 us (5%)
  matrix products  30.5 us (5%)
  local copies, waits for them, and re-layouts  27.5 us (4%)
  between operations  27.1 us (4%)
    ppermute x4, waiting for transfers between devices, try_all_plane_up(): n_now = ppermute(row_out, device_axis, line_up)  311 us
    unnamed x5, waiting for transfers between devices  115 us
    psum x1, blocking collectives, on_device(): lax.psum((jnp.sum(adam * adam, axis=(1, 2)), jnp.sum(direction * directio...  32.2 us
    psum x1, waiting for transfers between devices, on_device(): grad_rows = lax.psum(partial_rows, 'shard')  29.1 us
    psum x1, waiting for transfers between devices, spread(): return lax.psum(kept, axis)  22.4 us
    unnamed x48, local copies, waits for them, and re-layouts  14.7 us
  transfers between devices with their start and end apart: 8, of which 7 were waited for; matrix products, arithmetic and copies ran while one was open for 8% of the time, Pallas kernels for 0%

profile of v1, /device:TPU:0, one launch (start us, length us, event | category | flops | bytes accessed | tf_op | source)
XLA Modules:
  0.0 632.7 jit_solution(13185630271887620476)
XLA Ops:
  7.2 2.4 fusion.108
  9.6 2.1 fusion.111
  11.8 0.8 fusion.114
  12.6 0.8 fusion.117
  13.4 4.0 maximum_multiply_fusion
  17.5 9.6 %copy.23 = f32[768,3072]{1,0:T(8,128)} copy(f32[768,3072]{0,1:T(8,128)} %maximum_multiply_fusion) | data formatting | bytes 18874368
  27.2 114.2 %reduce-scatter.4.cloned.1.call-done = f32[48,3072]{1,0:T(8,128)} async-done(((f32[768,3072]{1,0:T(8,128)}), f32[48,3072]{1,0:T(8,128)}) %reduce-scatter.4.cloned.1.call-update) | async-done | bytes 589840
  141.3 1.5 copy.24
  142.9 1.3 copy.19
  144.2 0.7 all-gather.2.cloned.1.call-update
  145.0 0.1 broadcast_compare_fusion
  145.1 29.1 %all-reduce.5.cloned.1.call-done = f32[48,4,768]{2,0,1:T(8,128)} async-done(((f32[48,4,768]{2,0,1:T(8,128)}), f32[48,4,768]{2,0,1:T(8,128)}) %all-reduce.5.cloned.1.call-update) | async-done | bytes 589840 | tf_op jit(solution)/shard_map/psum | solution.py:84
  174.1 1.6 gather_fusion.1
  175.8 1.0 fusion.134
  176.8 2.0 collective-permute-done
  178.8 0.1 broadcast_select_fusion.8
  178.9 1.1 pad_maximum_fusion.2
  180.0 1.5 collective-permute-start.1
  181.5 33.1 %collective-permute-done.1 = f32[2,4,48,768]{3,2,1,0:T(8,128)S(1)} collective-permute-done((f32[2,4,48,768]{3,2,1,0:T(8,128)}, f32[2,4,48,768]{3,2,1,0:T(8,128)S(1)}, u32[]{:S(2)}, u32[]{:S(2)}) %collective-permute-start.1) | collective-permute-done | bytes 1179680 | tf_op jit(solution)/shard_map/ppermute | solution.py:27
  214.6 0.2 broadcast_select_fusion.5
  214.8 0.2 pad_maximum_fusion.1
  215.1 0.8 copy-done.3
  215.8 0.6 copy-done.4
  216.4 1.4 collective-permute-start.2
  217.8 88.5 %collective-permute-done.2 = f32[4,4,48,768]{3,2,1,0:T(8,128)} collective-permute-done((f32[4,4,48,768]{3,2,1,0:T(8,128)S(1)}, f32[4,4,48,768]{3,2,1,0:T(8,128)}, u32[]{:S(2)}, u32[]{:S(2)}) %collective-permute-start.2) | collective-permute-done | bytes 2359328 | tf_op jit(solution)/shard_map/ppermute | solution.py:27
  306.3 2.8 broadcast_select_fusion.3
  309.1 2.8 pad_maximum_fusion
  312.0 2.4 collective-permute-start.3
  314.4 0.7 fusion.135
  325.4 0.7 fusion.140
  328.7 1.3 gather_fusion
  329.9 187.8 %collective-permute-done.3 = f32[8,4,48,768]{3,2,1,0:T(8,128)} collective-permute-done((f32[8,4,48,768]{3,2,1,0:T(8,128)}, f32[8,4,48,768]{3,2,1,0:T(8,128)}, u32[]{:S(2)}, u32[]{:S(2)}) %collective-permute-start.3) | collective-permute-done | bytes 4718624 | tf_op jit(solution)/shard_map/ppermute | solution.py:27
  517.8 7.6 %broadcast_select_fusion.1 = (f32[8,4,48,768]{3,2,1,0:T(8,128)}, f32[8,4,48,768]{3,2,1,0:T(8,128)}) fusion(f32[8,4,48,768]{3,2,1,0:T(8,128)} %collective-permute-done.3, pred[]{:T(512)S(6)} %eq.43, f32[4,4,48,768]{3,2,1,0:T(8,128)} %copy-done.2, f32[4,4,48,768]{3,2,1,0:T(8,128)S(1)} %get-tuple-element.141), kind=kLoop, calls=%fused_computation.91 | loop fusion | flops 3538944 | bytes 18874368 | tf_op jit(solution)/shard_map/jit(_where)/select_n | solution.py:30
  525.4 4.4 maximum_bitcast_fusion
  529.8 4.2 copy.20
  534.0 0.2 conditional.8
  534.3 0.6 copy-done.14
  534.9 0.1 copy-done.15
  535.0 10.8 %conditional.10 = (f32[48,768]{1,0:T(8,128)S(1)}, f32[1,48,768]{2,1,0:T(8,128)S(1)}, f32[1,48,768]{2,1,0:T(8,128)S(1)}) conditional(s32[]{:T(128)} %bitcast.45, () %tuple.93, (f32[4,48,768]{2,1,0:T(8,128)}, f32[4,768,768]{2,1,0:T(8,128)}, f32[4,48,768]{2,1,0:T(8,128)}, s32[]{:T(128)}) %tuple.151), branch_computations={%region_9.10_spmd, %region_10.11_spmd} | conditional | flops 1019215872 | bytes 12927038 | solution.py:101
  535.0 1.8 slice.65
  536.8 1.7 fusion.36
  538.5 3.3 fusion.31
  541.8 4.0 fusion.33
  545.8 0.6 copy-done.16
  546.4 0.1 copy-done.17
  546.5 0.3 conditional.12
  546.8 0.6 copy-done.18
  547.5 10.8 %conditional.14 = (f32[48,768]{1,0:T(8,128)S(1)}, f32[1,48,768]{2,1,0:T(8,128)S(1)}, f32[1,48,768]{2,1,0:T(8,128)S(1)}) conditional(s32[]{:T(128)} %bitcast.47, () %tuple.99, (f32[4,48,768]{2,1,0:T(8,128)}, f32[4,768,768]{2,1,0:T(8,128)}, f32[4,48,768]{2,1,0:T(8,128)}, s32[]{:T(128)}) %tuple.153), branch_computations={%region_17.18_spmd, %region_18.19_spmd} | conditional | flops 1019215872 | bytes 12927038 | solution.py:101
  547.5 1.8 slice.73
  549.3 1.7 fusion.90
  551.0 3.3 fusion.85
  554.3 4.0 fusion.87
  558.4 3.2 conditional.11
  558.4 3.2 fusion.51
  561.7 0.3 conditional.9
  562.0 3.3 conditional.15
  562.1 3.3 fusion.105
  565.4 0.2 multiply_reduce_fusion
  565.6 3.3 fusion.133
  568.9 32.2 %all-reduce = (f32[4]{0:T(128)S(1)}, f32[4]{0:T(128)S(1)}) all-reduce(f32[4]{0:T(128)S(1)} %multiply_reduce_fusion, f32[4]{0:T(128)S(1)} %get-tuple-element.146), channel_id=1, replica_groups=mesh['shard'=2,'tensor'=4,'section'=4] {'tensor','section'}, use_global_device_ids=true, to_apply=%region_22.23 | all-reduce | flops 8 | bytes 64 | tf_op jit(solution)/shard_map/psum | solution.py:130
  601.1 0.2 subtract_convert_fusion
  601.2 0.7 dynamic-slice_select_fusion.3
  602.0 22.4 %all-reduce.7.cloned.1.call-done = (bf16[1,48,768]{2,1,0:T(8,128)(2,1)}, bf16[1,48,768]{2,1,0:T(8,128)(2,1)}, bf16[1,48,768]{2,1,0:T(8,128)(2,1)}, bf16[1,48,768]{2,1,0:T(8,128)(2,1)}) async-done(((bf16[1,48,768]{2,1,0:T(8,128)(2,1)}, bf16[1,48,768]{2,1,0:T(8,128)(2,1)}, bf16[1,48,768]{2,1,0:T(8,128)(2,1)}, bf16[1,48,768]{2,1,0:T(8,128)(2,1)}), (bf16[1,48,768]{2,1,0:T(8,128)(2,1)}, ...) | async-done | bytes 294928 | tf_op jit(solution)/shard_map/psum | solution.py:38
  624.4 1.7 pad_maximum_fusion.4
  (59 shorter events, 0.6 us)
Async XLA Ops:
  7.2 321.5 %copy-start = (bf16[4,48,768]{2,1,0:T(8,128)(2,1)S(1)}, bf16[4,48,768]{2,1,0:T(8,128)(2,1)}, u32[]{:S(2)}) copy-start(bf16[4,48,768]{2,1,0:T(8,128)(2,1)} %param.28) | copy-start | bytes 884740
  7.2 2.4 copy-start.7
  7.2 134.2 %reduce-scatter.4.cloned.1.call-start = ((), (), s32[]{:S(2)}) async-start(), calls=%async_computation.3 | async-start | bytes 10027008
  9.6 2.1 copy-start.8
  27.1 117.9 %copy-start.22 = (s32[8]{0:T(128)S(1)}, s32[8]{0:T(128)}, u32[]{:S(2)}) copy-start(s32[8]{0:T(128)} %param.29) | copy-start | bytes 100
  27.1 147.0 %all-reduce.5.cloned.1.call-start = ((), (), s32[]{:S(2)}) async-start(), calls=%async_computation.1 | async-start | bytes 1179648 | tf_op jit(solution)/shard_map/psum | solution.py:84
  142.9 32.9 %copy-start.9 = (f32[4,48,768]{2,1,0:T(8,128)S(1)}, f32[4,48,768]{2,1,0:T(8,128)}, u32[]{:S(2)}) copy-start(f32[4,48,768]{2,1,0:T(8,128)} %param.35) | copy-start | bytes 1769476
  144.2 414.2 %all-gather.2.cloned.1.call-start = ((), (), s32[]{:S(2)}) async-start(), calls=%async_computation.2 | async-start | bytes 10027008 | tf_op jit(solution)/shard_map/all_gather | solution.py:115
  144.9 479.5 %all-reduce.7.cloned.1.call-start = ((), (), s32[]{:S(2)}) async-start(), calls=%async_computation.4 | async-start | bytes 589824 | tf_op jit(solution)/shard_map/psum | solution.py:38
  176.8 3.2 copy-start.5
  176.8 2.0 collective-permute-start
  180.0 34.5 %collective-permute-start.1 = (f32[2,4,48,768]{3,2,1,0:T(8,128)}, f32[2,4,48,768]{3,2,1,0:T(8,128)S(1)}, u32[]{:S(2)}, u32[]{:S(2)}) collective-permute-start(f32[2,4,48,768]{3,2,1,0:T(8,128)} %pad_maximum_fusion.2), channel_id=1, source_target_pairs={{0,2},{1,3},{2,0},{3,1},{4,6},{5,7},{6,4},{7,5},{8,10},{9,11},{10,... | collective-permute-start | bytes 3538952 | tf_op jit(solution)/shard_map/ppermute | solution.py:27
  214.8 1.0 copy-start.3
  214.8 1.6 copy-start.4
  216.4 89.9 %collective-permute-start.2 = (f32[4,4,48,768]{3,2,1,0:T(8,128)S(1)}, f32[4,4,48,768]{3,2,1,0:T(8,128)}, u32[]{:S(2)}, u32[]{:S(2)}) collective-permute-start(f32[4,4,48,768]{3,2,1,0:T(8,128)S(1)} %pad_maximum_fusion.1), channel_id=1, source_target_pairs={{0,4},{1,5},{2,6},{3,7},{4,0},{5,1},{6,2},{7,3},{8,12},{9,13},{10,... | collective-permute-start | bytes 7077896 | tf_op jit(solution)/shard_map/ppermute | solution.py:27
  309.1 2.9 copy-start.2
  312.0 205.8 %collective-permute-start.3 = (f32[8,4,48,768]{3,2,1,0:T(8,128)}, f32[8,4,48,768]{3,2,1,0:T(8,128)}, u32[]{:S(2)}, u32[]{:S(2)}) collective-permute-start(f32[8,4,48,768]{3,2,1,0:T(8,128)} %pad_maximum_fusion), channel_id=1, source_target_pairs={{0,8},{1,9},{2,10},{3,11},{4,12},{5,13},{6,14},{7,15},{8,0},{9,1},... | collective-permute-start | bytes 14155784 | tf_op jit(solution)/shard_map/ppermute | solution.py:27
  534.3 0.7 copy-start.14
  534.3 0.7 copy-start.15
  545.8 0.7 copy-start.16
  545.8 0.7 copy-start.17
  546.8 0.6 copy-start.18
  546.8 0.7 copy-start.19
  558.3 3.3 copy-start.20
  558.3 3.3 copy-start.21
  562.0 3.5 copy-start.6
  562.0 3.5 copy-start.10
  562.0 3.5 copy-start.12
  562.0 3.5 copy-start.13
  565.5 35.5 %copy-start.11 = (bf16[4,48,768]{2,1,0:T(8,128)(2,1)S(1)}, bf16[4,48,768]{2,1,0:T(8,128)(2,1)}, u32[]{:S(2)}) copy-start(bf16[4,48,768]{2,1,0:T(8,128)(2,1)} %gather_fusion) | copy-start | bytes 884740
  565.6 60.6 %copy-start.1 = (bf16[4,48,768]{2,1,0:T(8,128)(2,1)S(1)}, bf16[4,48,768]{2,1,0:T(8,128)(2,1)}, u32[]{:S(2)}) copy-start(bf16[4,48,768]{2,1,0:T(8,128)(2,1)} %param.28) | copy-start | bytes 884740
Sparse Core Ops, SparseCore 0:
  27.2 114.0 reduce-scatter.3
  144.3 29.7 all-reduce.4
  176.4 112.9 all-gather.1
  602.1 22.2 all-reduce.6
